TPU v7x, 32 devices: a whole 2x2x4 slice. The times are simulated.
32 devices in a mesh: wide: 16 (over z, y, core), narrow: 2 (over x).
Axes of the slice: x: 2, y: 2, z: 4, core: 2. Of those that a mesh axis runs over, the one named last changes fastest.
Arguments:
- grid: bfloat16 [192, 256, 1440], P('wide', 'narrow'), may hold values from -6 to 6
- quad_weights: float32 [192], P('wide'), may hold values from 0.25 to 2
- orders: int32 [32], replicated, may hold values from 0 to 719, as said below
- legendre: bfloat16 [32, 720, 192], P('wide'), as said below
- mix_real: bfloat16 [256, 256], replicated, may hold values from -0.25 to 0.25
- mix_imag: bfloat16 [256, 256], replicated, may hold values from -0.25 to 0.25
- filter_gain: bfloat16 [720, 256], replicated, may hold values from 0.25 to 4
Outputs:
- field_out: bfloat16 [192, 256, 1440], P('wide', 'narrow')
Inputs may be any that keep to these rules, and one draw needn't show every extreme that they name: `orders`: every order appears in one slot only; slots 2 q and 2 q + 1 hold p and 719 - p for some p below 360, so the 2 slots of a device come in such pairs. legendre[k, l, :] is zero for every degree l below orders[k].
All inputs are finite; a program needn't handle non-finite values.
Results may differ from a plain program's by a relative error of at most 0.007.
Values may be sent and summed in bfloat16 or wider, within the bound.
A program may use at most 64 MiB of HBM per device.

v0:
```python
import math

import jax
import jax.numpy as jnp
from jax import lax
from jax.sharding import PartitionSpec as P


def fourier_tables(orders, lon_count):
    columns = jnp.arange(lon_count, dtype=jnp.int32)
    phase_int = orders[:, None] * columns[None, :] % lon_count
    angles = phase_int.astype(jnp.float32) * (2.0 * math.pi / lon_count)
    return (jnp.cos(angles).astype(jnp.bfloat16), jnp.sin(angles).astype(jnp.bfloat16))


def shards(grid, quad_weights, orders, legendre, mix_real, mix_imag, filter_gain):
    lon_count = grid.shape[2]
    order_count = orders.shape[0]
    cosine_table, sine_table = fourier_tables(orders, lon_count)
    factor = 1.0 / math.sqrt(lon_count)
    real_part = (
        jnp.einsum("acn,kn->kac", grid, cosine_table, preferred_element_type=jnp.float32) * factor
    )
    imag_part = (
        -jnp.einsum("acn,kn->kac", grid, sine_table, preferred_element_type=jnp.float32) * factor
    )
    spectra = (
        jnp.stack([real_part, imag_part], axis=2) * quad_weights[None, :, None, None]
    ).astype(jnp.bfloat16)
    by_order = lax.all_to_all(spectra, "wide", split_axis=0, concat_axis=1, tiled=True)
    m_dev = by_order.shape[0]
    lat_count = by_order.shape[1]
    chan_dev = by_order.shape[3]
    deg_count = legendre.shape[1]
    coeffs = jnp.einsum(
        "mlx,mxk->mlk",
        legendre,
        by_order.reshape(m_dev, lat_count, 2 * chan_dev),
        preferred_element_type=jnp.float32,
    )
    coeffs = coeffs.astype(jnp.bfloat16).reshape(m_dev, deg_count, 2, chan_dev)
    deg_dev = deg_count // lax.axis_size("narrow")
    gain_rows = lax.dynamic_slice_in_dim(
        filter_gain, lax.axis_index("narrow") * deg_dev, deg_dev, 0
    ).astype(jnp.float32)
    upper = jnp.concatenate([mix_real, mix_imag], axis=1)
    lower = jnp.concatenate([-mix_imag, mix_real], axis=1)
    wide_block = jnp.concatenate([upper, lower], axis=0)
    fragment = lax.all_to_all(coeffs, "narrow", split_axis=1, concat_axis=3, tiled=True)
    frag_count = fragment.shape[0]
    chan_all = fragment.shape[3]
    flat_rows = fragment.reshape(frag_count * deg_dev, 2 * chan_all)
    product = jnp.dot(flat_rows, wide_block, preferred_element_type=jnp.float32)
    product = product.reshape(frag_count, deg_dev, 2, chan_all) * gain_rows[None, :, None, :]
    mixed_coeffs = product.astype(jnp.bfloat16)
    back_coeffs = lax.all_to_all(mixed_coeffs, "narrow", split_axis=3, concat_axis=1, tiled=True)
    synthesis = jnp.einsum(
        "mlx,mlk->mxk",
        legendre,
        back_coeffs.reshape(m_dev, deg_count, 2 * chan_dev),
        preferred_element_type=jnp.float32,
    )
    synthesis = synthesis.astype(jnp.bfloat16).reshape(m_dev, lat_count, 2, chan_dev)
    by_latitude = lax.all_to_all(synthesis, "wide", split_axis=1, concat_axis=0, tiled=True)
    field_out = jnp.einsum(
        "kac,kn->acn", by_latitude[:, :, 0], cosine_table, preferred_element_type=jnp.float32
    )
    field_out = field_out - jnp.einsum(
        "kac,kn->acn", by_latitude[:, :, 1], sine_table, preferred_element_type=jnp.float32
    )
    return (field_out / math.sqrt(order_count)).astype(jnp.bfloat16)


def solution(mesh):
    placed = (P("wide", "narrow", None), P("wide"), P(), P("wide", None, None), P(), P(), P())
    return jax.shard_map(
        shards, mesh=mesh, in_specs=placed, out_specs=P("wide", "narrow", None), check_vma=False
    )
```

profile of v0, /device:TPU:0, one launch (start us, length us, event | category | flops | bytes accessed | tf_op | source)
XLA Modules:
  0.0 74.2 jit_solution(16836718324196516378)
XLA Ops:
  0.0 0.0 copy-start
  0.0 0.0 copy-start.5
  0.0 0.0 copy-start.1
  0.0 0.0 copy-start.6
  0.0 3.9 %fusion.2 = f32[32,12,1,128]{3,0,1,2:T(8,128)S(1)} fusion(bf16[12,128,1440]{1,2,0:T(8,128)(2,1)} %param.7, s32[32]{0:T(128)} %param.9), kind=kOutput, calls=%fused_computation.7 | convolution fusion | flops 142116864 | bytes 4620416 | tf_op jit(solution)/shard_map/acn,kn->kac/dot_general | solution.py:25
  3.9 0.0 copy-done.5
  3.9 0.0 copy-done.1
  3.9 1.4 %fusion.3 = f32[32,12,1,128]{3,0,1,2:T(8,128)S(1)} fusion(bf16[12,128,1440]{1,2,0:T(8,128)(2,1)S(1)} %copy-done.1, s32[32]{0:T(128)S(1)} %copy-done.5), kind=kOutput, calls=%fused_computation.9 | convolution fusion | flops 142067712 | bytes 4620416 | tf_op jit(solution)/shard_map/acn,kn->kac/dot_general | solution.py:22
  5.3 0.0 copy-done.6
  5.3 0.0 copy-start.2
  5.4 0.0 copy-start.3
  5.4 0.1 fusion.6
  5.5 0.2 copy.22
  5.7 16.2 %all_to_all.63 = bf16[32,12,2,128]{3,2,1,0:T(2,128)(2,1)S(1)} all-to-all(bf16[32,12,2,128]{3,2,1,0:T(2,128)(2,1)S(1)} %copy.22), channel_id=1, replica_groups=mesh['wide'=16,'narrow'=2] {'wide'}, dimensions={0} | all-to-all | bytes 393216 | tf_op jit(solution)/shard_map/all_to_all | solution.py:30
  21.9 0.0 copy-start.4
  21.9 0.1 copy.35
  22.0 0.1 reshape.23
  22.2 0.0 copy-done
  22.2 0.4 fusion
  22.6 0.2 reshape.24
  22.8 1.4 %copy.24 = bf16[2,720,2,128]{3,2,0,1:T(2,128)(2,1)} copy(bf16[2,720,2,128]{3,2,1,0:T(2,128)(2,1)S(1)} %reshape.24) | data formatting | bytes 1474560 | tf_op jit(solution)/shard_map/reshape | solution.py:41
  24.2 3.5 %all-to-all-start.1 = ((bf16[2,720,2,128]{3,2,0,1:T(2,128)(2,1)}), bf16[2,720,2,128]{3,2,0,1:T(2,128)(2,1)S(1)}, u32[]{:S(2)}, u32[]{:S(2)}) async-start(bf16[2,720,2,128]{3,2,0,1:T(2,128)(2,1)} %copy.24), calls=%async_computation.1 | async-start | bytes 1474560 | tf_op jit(solution)/shard_map/all_to_all | solution.py:49
  27.7 0.0 copy-done.2
  27.7 0.0 copy-done.3
  27.8 0.2 copy.26
  28.0 0.0 copy-done.4
  28.1 10.0 %all-to-all-done.1 = bf16[2,720,2,128]{3,2,0,1:T(2,128)(2,1)S(1)} async-done(((bf16[2,720,2,128]{3,2,0,1:T(2,128)(2,1)}), bf16[2,720,2,128]{3,2,0,1:T(2,128)(2,1)S(1)}, u32[]{:S(2)}, u32[]{:S(2)}) %all-to-all-start.1) | async-done | bytes 737312 | tf_op jit(solution)/shard_map/all_to_all | solution.py:49
  38.1 0.8 %copy.34 = bf16[2,2,360,2,128]{4,1,3,2,0:T(2,128)(2,1)S(1)} copy(bf16[2,2,360,2,128]{4,3,0,2,1:T(2,128)(2,1)S(1)} %bitcast.52) | data formatting | bytes 1474560 | tf_op jit(solution)/shard_map/all_to_all | solution.py:49
  38.9 0.3 reshape.29
  39.2 0.6 multiply_convert_fusion.1
  39.8 1.2 %copy.27 = bf16[2,360,2,256]{1,2,0,3:T(2,128)(2,1)S(1)} copy(bf16[2,360,2,256]{3,1,2,0:T(8,128)(2,1)S(1)} %multiply_convert_fusion.1) | data formatting | bytes 1474560 | tf_op jit(solution)/shard_map/convert_element_type | solution.py:55
  41.0 12.5 %all_to_all.64 = bf16[2,360,2,256]{1,2,0,3:T(2,128)(2,1)S(1)} all-to-all(bf16[2,360,2,256]{1,2,0,3:T(2,128)(2,1)S(1)} %copy.27), channel_id=1, replica_groups=mesh['wide'=16,'narrow'=2] {'narrow'}, dimensions={3} | all-to-all | bytes 1474560 | tf_op jit(solution)/shard_map/all_to_all | solution.py:56
  53.5 1.0 %copy.28 = bf16[2,360,2,2,128]{4,2,1,3,0:T(2,128)(2,1)S(1)} copy(bf16[2,360,2,2,128]{1,2,0,4,3:T(2,128)(2,1)S(1)} %bitcast.51) | data formatting | bytes 1474560 | tf_op jit(solution)/shard_map/all_to_all | solution.py:56
  54.5 0.5 reshape.25
  55.0 0.3 fusion.4
  55.3 0.1 reshape.26
  55.3 0.1 copy.29
  55.5 12.3 %all_to_all.65 = bf16[2,192,2,128]{3,2,0,1:T(2,128)(2,1)S(1)} all-to-all(bf16[2,192,2,128]{3,2,0,1:T(2,128)(2,1)S(1)} %copy.29), channel_id=1, replica_groups=mesh['wide'=16,'narrow'=2] {'wide'}, dimensions={1} | all-to-all | bytes 393216 | tf_op jit(solution)/shard_map/all_to_all | solution.py:64
  67.8 0.1 copy.30
  67.9 2.0 %fusion.14 = f32[12,128,1440]{1,2,0:T(8,128)S(1)} fusion(bf16[32,12,2,128]{3,0,1,2:T(8,128)(2,1)S(1)} %bitcast.59, s32[32]{0:T(128)S(1)} %copy-done.5), kind=kOutput, calls=%fused_computation.31 | convolution fusion | flops 142018560 | bytes 8946176 | tf_op jit(solution)/shard_map/kac,kn->acn/dot_general | solution.py:65
  69.9 4.3 %multiply_convert_fusion = bf16[12,128,1440]{1,2,0:T(8,128)(2,1)} fusion(f32[12,128,1440]{1,2,0:T(8,128)S(1)} %fusion.14, bf16[32,12,2,128]{3,0,1,2:T(8,128)(2,1)S(1)} %bitcast.60, s32[32]{0:T(128)S(1)} %copy-done.5), kind=kOutput, calls=%fused_computation | convolution fusion | flops 148654080 | bytes 13369856 | tf_op jit(solution)/shard_map/kac,kn->acn/dot_general | solution.py:68
  (3 shorter events, 0.1 us)
Async XLA Ops:
  0.0 22.2 %copy-start = (bf16[2,720,192]{1,2,0:T(8,128)(2,1)S(1)}, bf16[2,720,192]{1,2,0:T(8,128)(2,1)}, u32[]{:S(2)}) copy-start(bf16[2,720,192]{1,2,0:T(8,128)(2,1)} %param.10) | copy-start | bytes 1658884
  0.0 3.9 %copy-start.5 = (s32[32]{0:T(128)S(1)}, s32[32]{0:T(128)}, u32[]{:S(2)}) copy-start(s32[32]{0:T(128)} %param.9) | copy-start | bytes 388
  0.0 3.9 %copy-start.1 = (bf16[12,128,1440]{1,2,0:T(8,128)(2,1)S(1)}, bf16[12,128,1440]{1,2,0:T(8,128)(2,1)}, u32[]{:S(2)}) copy-start(bf16[12,128,1440]{1,2,0:T(8,128)(2,1)} %param.7) | copy-start | bytes 13271044
  0.0 5.3 %copy-start.6 = (f32[12]{0:T(128)S(1)}, f32[12]{0:T(128)}, u32[]{:S(2)}) copy-start(f32[12]{0:T(128)} %param.8) | copy-start | bytes 148
  5.3 22.4 %copy-start.2 = (bf16[256,256]{1,0:T(8,128)(2,1)S(1)}, bf16[256,256]{1,0:T(8,128)(2,1)}, u32[]{:S(2)}) copy-start(bf16[256,256]{1,0:T(8,128)(2,1)} %param.12) | copy-start | bytes 393220
  5.4 22.4 %copy-start.3 = (bf16[256,256]{1,0:T(8,128)(2,1)S(1)}, bf16[256,256]{1,0:T(8,128)(2,1)}, u32[]{:S(2)}) copy-start(bf16[256,256]{1,0:T(8,128)(2,1)} %param.11) | copy-start | bytes 393220
  21.9 6.1 %copy-start.4 = (bf16[720,256]{1,0:T(8,128)(2,1)S(1)}, bf16[720,256]{1,0:T(8,128)(2,1)}, u32[]{:S(2)}) copy-start(bf16[720,256]{1,0:T(8,128)(2,1)} %param.13) | copy-start | bytes 1105924
  24.2 14.0 %all-to-all-start.1 = ((bf16[2,720,2,128]{3,2,0,1:T(2,128)(2,1)}), bf16[2,720,2,128]{3,2,0,1:T(2,128)(2,1)S(1)}, u32[]{:S(2)}, u32[]{:S(2)}) async-start(bf16[2,720,2,128]{3,2,0,1:T(2,128)(2,1)} %copy.24), calls=%async_computation.1 | async-start | bytes 1474560 | tf_op jit(solution)/shard_map/all_to_all | solution.py:49
where the time goes:
time: 74.5 us; the launch traced here: 74.2 us
  blocking collectives  41 us (55%)
  matrix products  12.9 us (17%)
  waiting for transfers between devices  10 us (13%)
  local copies, waits for them, and re-layouts  6.25 us (8%)
  starting transfers between devices  3.53 us (5%)
    all_to_all x1, blocking collectives, shards(): lax.all_to_all(spectra, 'wide', split_axis=0, concat_axis=1, tiled=True)  16.2 us
    all_to_all x1, blocking collectives, shards(): lax.all_to_all(mixed_coeffs, 'narrow', split_axis=3, concat_axis=1, tiled...  12.5 us
    all_to_all x1, blocking collectives, shards(): lax.all_to_all(synthesis, 'wide', split_axis=1, concat_axis=0, tiled=True)  12.3 us
    all_to_all x1, waiting for transfers between devices, shards(): lax.all_to_all(coeffs, 'narrow', split_axis=1, concat_axis=3, tiled=True)  10 us
    dot_general x1, matrix products, shards(): jnp.einsum('kac,kn->acn', by_latitude[:, :, 1], sine_table, preferred_ele...  4.27 us
    dot_general x1, matrix products, shards(): jnp.einsum('acn,kn->kac', grid, sine_table, preferred_element_type=jnp.fl...  3.86 us
    all_to_all x1, starting transfers between devices, shards(): lax.all_to_all(coeffs, 'narrow', split_axis=1, concat_axis=3, tiled=True)  3.53 us
    dot_general x1, matrix products, shards(): jnp.einsum('kac,kn->acn', by_latitude[:, :, 0], cosine_table, preferred_e...  2.01 us
  transfers between devices with their start and end apart: 1, of which 1 were waited for; matrix products, arithmetic and copies ran while one was open for 0% of the time, Pallas kernels for 0%

commit v1 on v0

--- a/solution.py
+++ b/solution.py
@@ -1,9 +1,16 @@
+import functools
 import math
 
 import jax
 import jax.numpy as jnp
 from jax import lax
+from jax.experimental import pallas as pl
+from jax.experimental.pallas import tpu as pltpu
 from jax.sharding import PartitionSpec as P
+
+MESH = pl.DeviceIdType.MESH
+SUB = 8
+LANES = 128
 
 
 def fourier_tables(orders, lon_count):
@@ -13,7 +20,7 @@
     return (jnp.cos(angles).astype(jnp.bfloat16), jnp.sin(angles).astype(jnp.bfloat16))
 
 
-def shards(grid, quad_weights, orders, legendre, mix_real, mix_imag, filter_gain):
+def general_shards(grid, quad_weights, orders, legendre, mix_real, mix_imag, filter_gain):
     lon_count = grid.shape[2]
     order_count = orders.shape[0]
     cosine_table, sine_table = fourier_tables(orders, lon_count)
@@ -71,6 +78,369 @@
     return (field_out / math.sqrt(order_count)).astype(jnp.bfloat16)
 
 
+def turn_cosine(phase, period):
+    quarter = period // 4
+    turns = jnp.floor(phase * (1.0 / quarter) + 0.5)
+    angle = (phase - turns * quarter) * (2.0 * math.pi / period)
+    quadrant = turns - 4.0 * jnp.floor(turns * 0.25)
+    sq = angle * angle
+    cosine = 1.0 + sq * (-0.5 + sq * (1.0 / 24 + sq * (-1.0 / 720 + sq * (1.0 / 40320))))
+    sine = angle * (1.0 + sq * (-1.0 / 6 + sq * (1.0 / 120 + sq * (-1.0 / 5040 + sq * (1.0 / 362880)))))
+    odd = (quadrant == 1.0) | (quadrant == 3.0)
+    flip = (quadrant == 1.0) | (quadrant == 2.0)
+    value = jnp.where(odd, sine, cosine)
+    return jnp.where(flip, -value, value)
+
+
+def spectral_kernel(
+    dims, orders_ref, quad_ref, grid_hbm, leg_hbm, mixr_hbm, mixi_hbm, gain_hbm,
+    out_ref, tabt_ref,
+    grid_v, leg_v, mixr_v, mixi_v, gain_v, tab, spread_a, spread_b, send1, recv1, lt, lf,
+    weight, mixed, send2, recv2, flat2,
+    grid_sem, in_sem, local_sem, s_send, s_recv, f_send, f_recv, b_send, b_recv,
+):
+    n_wide, lat_dev, lon_count, chan, m_dev, deg_count = dims
+    order_count = n_wide * m_dev
+    rows = 2 * order_count
+    rest = lat_dev - SUB
+    parts = m_dev + 1
+    half = n_wide * SUB
+    pairs = lat_dev // 2
+    me = lax.axis_index("wide")
+    x = lax.axis_index("narrow")
+    partner = 1 - x
+
+    grid_copies = []
+    for p in range(pairs):
+        copy = pltpu.make_async_copy(
+            grid_hbm.at[pl.ds(2 * p, 2)], grid_v.at[pl.ds(2 * p, 2)], grid_sem.at[p]
+        )
+        copy.start()
+        grid_copies.append(copy)
+    in_copies = []
+    for i, (src, dst) in enumerate(
+        ((leg_hbm, leg_v), (mixr_hbm, mixr_v), (mixi_hbm, mixi_v), (gain_hbm, gain_v))
+    ):
+        copy = pltpu.make_async_copy(src, dst, in_sem.at[i])
+        copy.start()
+        in_copies.append(copy)
+
+    barrier = pltpu.get_barrier_semaphore()
+    for d in range(1, n_wide):
+        pl.semaphore_signal(
+            barrier, inc=1, device_id=((me + d) % n_wide, x), device_id_type=MESH
+        )
+    pl.semaphore_signal(barrier, inc=1, device_id=(me, partner), device_id_type=MESH)
+
+    row = lax.broadcasted_iota(jnp.int32, (rows, LANES), 0)
+    lane = lax.broadcasted_iota(jnp.int32, (rows, LANES), 1)
+    block_rows = 2 * n_wide
+    order_row = jnp.zeros((rows, LANES), jnp.int32)
+    for j in range(m_dev):
+        for w in range(n_wide):
+            slot = orders_ref[w * m_dev + j]
+            hit = (row == j * block_rows + w) | (row == j * block_rows + n_wide + w)
+            order_row = jnp.where(hit, slot, order_row)
+    shift = jnp.zeros((rows, LANES), jnp.int32)
+    for j in range(m_dev):
+        low = j * block_rows + n_wide
+        shift = jnp.where((row >= low) & (row < low + n_wide), lon_count // 4, shift)
+    for start in range(0, lon_count, LANES):
+        size = min(LANES, lon_count - start)
+        phase = (order_row * (lane + start) + shift).astype(jnp.float32)
+        value = turn_cosine(phase, lon_count)
+        tab[:, start:start + size] = value.astype(jnp.bfloat16)[:, :size]
+        tabt_ref[start:start + size, :] = jnp.transpose(value)[:size].astype(jnp.bfloat16)
+
+    factor = 1.0 / math.sqrt(lon_count)
+
+    def transform(p):
+        grid_copies[p].wait()
+        rhs = jnp.concatenate([grid_v[2 * p], grid_v[2 * p + 1]], axis=1)
+        res = jnp.dot(tab[...], rhs, preferred_element_type=jnp.float32)
+        for i in range(2):
+            a = 2 * p + i
+            part = res[:, i * chan:(i + 1) * chan] * (quad_ref[a] * factor)
+            if a < SUB:
+                spread_a[a * rows:(a + 1) * rows, :] = part
+            else:
+                for j in range(m_dev):
+                    at = (j * rest + a - SUB) * block_rows
+                    spread_b[at:at + block_rows, :] = part[j * block_rows:(j + 1) * block_rows]
+
+    def wide_copy(part, d):
+        to = (me + d) % n_wide
+        where = pl.ds(0, m_dev) if part == 0 else pl.ds(m_dev, 1)
+        return pltpu.make_async_remote_copy(
+            src_ref=send1.at[to, where],
+            dst_ref=recv1.at[0, me, where],
+            send_sem=s_send.at[part, d],
+            recv_sem=s_recv.at[part, me],
+            device_id=(to, x),
+            device_id_type=MESH,
+        )
+
+    def wide_arrival(part, src):
+        where = pl.ds(0, m_dev) if part == 0 else pl.ds(m_dev, 1)
+        return pltpu.make_async_remote_copy(
+            src_ref=send1.at[src, where],
+            dst_ref=recv1.at[0, src, where],
+            send_sem=s_send.at[part, 0],
+            recv_sem=s_recv.at[part, src],
+            device_id=(src, x),
+            device_id_type=MESH,
+        )
+
+    def forward_copy(part, src):
+        where = pl.ds(0, m_dev) if part == 0 else pl.ds(m_dev, 1)
+        return pltpu.make_async_remote_copy(
+            src_ref=recv1.at[0, src, where],
+            dst_ref=recv1.at[1, src, where],
+            send_sem=f_send.at[part, src],
+            recv_sem=f_recv.at[part, src],
+            device_id=(me, partner),
+            device_id_type=MESH,
+        )
+
+    def own_copy(part):
+        where = pl.ds(0, m_dev) if part == 0 else pl.ds(m_dev, 1)
+        return pltpu.make_async_copy(
+            send1.at[me, where], recv1.at[0, me, where], local_sem.at[part]
+        )
+
+    for p in range(SUB // 2):
+        transform(p)
+    for w in range(n_wide):
+        for j in range(m_dev):
+            for ri in range(2):
+                at = j * block_rows + ri * n_wide + w
+                send1[w, j, :, ri * chan:(ri + 1) * chan] = spread_a[
+                    pl.ds(at, SUB, stride=rows), :
+                ].astype(jnp.bfloat16)
+    pl.semaphore_wait(barrier, n_wide)
+    for d in range(1, n_wide):
+        wide_copy(0, d).start()
+    own_copy(0).start()
+
+    for p in range(SUB // 2, pairs):
+        transform(p)
+    for w in range(n_wide):
+        for ri in range(2):
+            send1[w, m_dev, :, ri * chan:(ri + 1) * chan] = spread_b[
+                pl.ds(ri * n_wide + w, SUB, stride=block_rows), :
+            ].astype(jnp.bfloat16)
+    for d in range(1, n_wide):
+        wide_copy(1, d).start()
+    own_copy(1).start()
+    for part in range(2):
+        own_copy(part).wait()
+        forward_copy(part, me).start()
+
+    for copy in in_copies:
+        copy.wait()
+    lat_count = n_wide * lat_dev
+    slot = lax.broadcasted_iota(jnp.int32, (2 * half, lat_count), 0)
+    lat = lax.broadcasted_iota(jnp.int32, (2 * half, lat_count), 1)
+    local = slot % SUB
+    device = jnp.where(slot < half, slot, slot - half) // SUB
+    for j in range(m_dev):
+        tail = jnp.where(
+            (local >= j * rest) & (local < (j + 1) * rest),
+            device * lat_dev + SUB + local - j * rest,
+            -1,
+        )
+        want = jnp.where(slot < half, device * lat_dev + local, tail)
+        pick = (want == lat).astype(jnp.bfloat16)
+        moved = jnp.dot(pick, leg_v[j], preferred_element_type=jnp.float32)
+        lt[j] = moved.astype(jnp.bfloat16)
+        lf[j] = jnp.transpose(moved).astype(jnp.bfloat16)
+    own_cols = pl.ds(pl.multiple_of(x * chan, chan), chan)
+    for i, who in enumerate((x, partner)):
+        in_rows = pl.ds(pl.multiple_of(who * chan, chan), chan)
+        re = mixr_v[in_rows, own_cols]
+        im = mixi_v[in_rows, own_cols]
+        top = 2 * i * chan
+        weight[top:top + chan, :chan] = re
+        weight[top:top + chan, chan:] = im
+        weight[top + chan:top + 2 * chan, :chan] = -im
+        weight[top + chan:top + 2 * chan, chan:] = re
+
+    for part in range(2):
+        for d in range(1, n_wide):
+            src = (me + n_wide - d) % n_wide
+            wide_arrival(part, src).wait_recv()
+            forward_copy(part, src).start()
+    for part in range(2):
+        for d in range(n_wide):
+            forward_copy(part, (me + n_wide - d) % n_wide).wait_recv()
+
+    gain = gain_v[:, own_cols].astype(jnp.float32)
+    gain = jnp.concatenate([gain, gain], axis=1)
+    tails = []
+    for j in range(m_dev):
+        sides = []
+        for side in range(2):
+            head = recv1[side, :, j].reshape(half, 2 * chan)
+            tail = recv1[side, :, m_dev].reshape(half, 2 * chan)
+            sides.append(jnp.concatenate([head, tail], axis=0))
+        spec = jnp.concatenate(sides, axis=1)
+        coeffs = jnp.dot(lf[j], spec, preferred_element_type=jnp.float32).astype(jnp.bfloat16)
+        product = jnp.dot(coeffs, weight[...], preferred_element_type=jnp.float32)
+        mixed[j] = (product * gain).astype(jnp.bfloat16)
+        syn = jnp.dot(lt[j], mixed[j], preferred_element_type=jnp.float32)
+        send2[:, j] = syn[:half].astype(jnp.bfloat16).reshape(n_wide, SUB, 2 * chan)
+        tails.append(syn[half:])
+    total = functools.reduce(lambda a, b: a + b, tails)
+    send2[:, m_dev] = total.astype(jnp.bfloat16).reshape(n_wide, SUB, 2 * chan)
+
+    def back_copy(to, d):
+        return pltpu.make_async_remote_copy(
+            src_ref=send2.at[to],
+            dst_ref=recv2.at[me],
+            send_sem=b_send.at[d],
+            recv_sem=b_recv.at[me],
+            device_id=(to, x),
+            device_id_type=MESH,
+        )
+
+    def back_arrival(src):
+        return pltpu.make_async_remote_copy(
+            src_ref=send2.at[src],
+            dst_ref=recv2.at[src],
+            send_sem=b_send.at[0],
+            recv_sem=b_recv.at[src],
+            device_id=(src, x),
+            device_id_type=MESH,
+        )
+
+    for d in range(1, n_wide):
+        back_copy((me + d) % n_wide, d).start()
+    own_back = pltpu.make_async_copy(send2.at[me], recv2.at[me], local_sem.at[2])
+    own_back.start()
+    for part in range(2):
+        for d in range(1, n_wide):
+            wide_copy(part, d).wait_send()
+        for d in range(n_wide):
+            forward_copy(part, (me + n_wide - d) % n_wide).wait_send()
+    own_back.wait()
+    for d in range(1, n_wide):
+        back_arrival((me + n_wide - d) % n_wide).wait_recv()
+    for ri in range(2):
+        flat2[ri] = recv2[:, :, :, ri * chan:(ri + 1) * chan].astype(jnp.float32).reshape(
+            n_wide * parts * SUB, chan
+        )
+    for a in range(lat_dev):
+        for j in range(m_dev):
+            for ri in range(2):
+                at = j * SUB + a if a < SUB else m_dev * SUB + j * rest + a - SUB
+                top = j * block_rows + ri * n_wide
+                out_ref[a, top:top + n_wide, :] = flat2[
+                    ri, pl.ds(at, n_wide, stride=parts * SUB), :
+                ].astype(jnp.bfloat16)
+    for d in range(1, n_wide):
+        back_copy((me + d) % n_wide, d).wait_send()
+
+
+def field_kernel(scale, chan, tabt_ref, syn_ref, out_ref):
+    rhs = jnp.concatenate([syn_ref[0], syn_ref[1]], axis=1)
+    res = jnp.dot(tabt_ref[...], rhs, preferred_element_type=jnp.float32) * scale
+    res = res.astype(jnp.bfloat16)
+    out_ref[0] = res[:, :chan]
+    out_ref[1] = res[:, chan:]
+
+
+def fast_shards(grid, quad_weights, orders, legendre, mix_real, mix_imag, filter_gain):
+    lat_dev, chan, lon_count = grid.shape
+    order_count = orders.shape[0]
+    m_dev, deg_count, lat_count = legendre.shape
+    n_wide = lax.axis_size("wide")
+    rows = 2 * order_count
+    parts = m_dev + 1
+    half = n_wide * SUB
+    bf16, f32 = jnp.bfloat16, jnp.float32
+    vmem = pl.BlockSpec(memory_space=pltpu.VMEM)
+    smem = pl.BlockSpec(memory_space=pltpu.SMEM)
+    hbm = pl.BlockSpec(memory_space=pl.ANY)
+    dims = (n_wide, lat_dev, lon_count, chan, m_dev, deg_count)
+    chan_all = mix_real.shape[0]
+    dma = pltpu.SemaphoreType.DMA
+    synthesis, table = pl.pallas_call(
+        functools.partial(spectral_kernel, dims),
+        out_shape=(
+            jax.ShapeDtypeStruct((lat_dev, rows, chan), bf16),
+            jax.ShapeDtypeStruct((lon_count, rows), bf16),
+        ),
+        in_specs=[smem, smem, hbm, hbm, hbm, hbm, hbm],
+        out_specs=(vmem, vmem),
+        scratch_shapes=[
+            pltpu.VMEM((lat_dev, lon_count, chan), bf16),
+            pltpu.VMEM((m_dev, lat_count, deg_count), bf16),
+            pltpu.VMEM((chan_all, chan_all), bf16),
+            pltpu.VMEM((chan_all, chan_all), bf16),
+            pltpu.VMEM((deg_count, chan_all), bf16),
+            pltpu.VMEM((rows, lon_count), bf16),
+            pltpu.VMEM((SUB * rows, chan), f32),
+            pltpu.VMEM(((lat_dev - SUB) * rows, chan), f32),
+            pltpu.VMEM((n_wide, parts, SUB, 2 * chan), bf16),
+            pltpu.VMEM((2, n_wide, parts, SUB, 2 * chan), bf16),
+            pltpu.VMEM((m_dev, 2 * half, deg_count), bf16),
+            pltpu.VMEM((m_dev, deg_count, 2 * half), bf16),
+            pltpu.VMEM((4 * chan, 2 * chan), bf16),
+            pltpu.VMEM((m_dev, deg_count, 2 * chan), bf16),
+            pltpu.VMEM((n_wide, parts, SUB, 2 * chan), bf16),
+            pltpu.VMEM((n_wide, parts, SUB, 2 * chan), bf16),
+            pltpu.VMEM((2, n_wide * parts * SUB, chan), f32),
+            dma((lat_dev // 2,)),
+            dma((4,)),
+            dma((3,)),
+            dma((2, n_wide)),
+            dma((2, n_wide)),
+            dma((2, n_wide)),
+            dma((2, n_wide)),
+            dma((n_wide,)),
+            dma((n_wide,)),
+        ],
+        compiler_params=pltpu.CompilerParams(
+            collective_id=0, has_side_effects=True, vmem_limit_bytes=40 * 2**20
+        ),
+        name="spectral",
+    )(
+        orders, quad_weights, jnp.transpose(grid, (0, 2, 1)), jnp.transpose(legendre, (0, 2, 1)),
+        mix_real, mix_imag, filter_gain,
+    )
+    field = pl.pallas_call(
+        functools.partial(field_kernel, 1.0 / math.sqrt(order_count), chan),
+        grid=(lat_dev // 2,),
+        out_shape=jax.ShapeDtypeStruct((lat_dev, lon_count, chan), bf16),
+        in_specs=[
+            pl.BlockSpec((lon_count, rows), lambda p: (0, 0)),
+            pl.BlockSpec((2, rows, chan), lambda p: (p, 0, 0)),
+        ],
+        out_specs=pl.BlockSpec((2, lon_count, chan), lambda p: (p, 0, 0)),
+        name="field",
+    )(table, synthesis)
+    return jnp.transpose(field, (0, 2, 1))
+
+
+def shards(grid, quad_weights, orders, legendre, mix_real, mix_imag, filter_gain):
+    lat_dev, chan, lon_count = grid.shape
+    m_dev = legendre.shape[0]
+    n_wide = lax.axis_size("wide")
+    rest = lat_dev - SUB
+    fits = (
+        lax.axis_size("narrow") == 2
+        and chan == LANES
+        and lon_count % 4 == 0
+        and rest > 0
+        and rest * m_dev == SUB
+        and lat_dev % 2 == 0
+        and n_wide % 16 == 0
+        and lon_count * lon_count < 2**24
+    )
+    body = fast_shards if fits else general_shards
+    return body(grid, quad_weights, orders, legendre, mix_real, mix_imag, filter_gain)
+
+
 def solution(mesh):
     placed = (P("wide", "narrow", None), P("wide"), P(), P("wide", None, None), P(), P(), P())
     return jax.shard_map(

time: 74.5 us -> 42.1 us (0.57)
  blocking collectives: 41 us -> 0 us
  Pallas kernels: 0 us -> 32.7 us
  matrix products: 12.9 us -> 0 us
  waiting for transfers between devices: 10 us -> 0 us
  starting transfers between devices: 3.53 us -> 0 us
  local copies, waits for them, and re-layouts: 6.25 us -> 8.82 us
    all_to_all x3 -> x0, blocking collectives: 41 us -> none  [the longest x1 16.2 us: shards(): lax.all_to_all(spectra, 'wide', split_axis=0, concat_axis=1, tiled=True)]
    pallas_call x0 -> x2, Pallas kernels: none -> 32.7 us  [the longest x1 27.3 us: fast_shards(): pl.pallas_call(functools.partial(spectral_kernel, dims), out_shape=(jax.S...]
    dot_general x7 -> x0, matrix products: 12.9 us -> none  [the longest x1 4.27 us: shards(): jnp.einsum('kac,kn->acn', by_latitude[:, :, 1], sine_table, preferred_ele...]
    all_to_all x1 -> x0, waiting for transfers between devices: 10 us -> none  [shards(): lax.all_to_all(coeffs, 'narrow', split_axis=1, concat_axis=3, tiled=True)]
    unnamed x14 -> x18, local copies, waits for them, and re-layouts: 0.05 us -> 8.82 us
    all_to_all x1 -> x0, starting transfers between devices: 3.53 us -> none  [shards(): lax.all_to_all(coeffs, 'narrow', split_axis=1, concat_axis=3, tiled=True)]
    reshape x6 -> x0, local copies, waits for them, and re-layouts: 2.33 us -> none  [the longest x2 1.54 us: shards(): coeffs = coeffs.astype(jnp.bfloat16).reshape(m_dev, deg_count, 2, chan_dev)]
    all_to_all x4 -> x0, local copies, waits for them, and re-layouts: 1.97 us -> none  [the longest x1 0.96 us: shards(): lax.all_to_all(mixed_coeffs, 'narrow', split_axis=3, concat_axis=1, tiled...]
  transfers between devices with their start and end apart: 1 -> 0, of which waited for: 1 -> 0; matrix products, arithmetic and copies ran while one was open for 0% -> 0% of each run, Pallas kernels for 0% -> 0%
where the time goes in v1:
time: 42.1 us; the launch traced here: 41.6 us
  Pallas kernels  32.7 us (78%)
  local copies, waits for them, and re-layouts  8.82 us (21%)
    pallas_call x1, Pallas kernels, fast_shards(): pl.pallas_call(functools.partial(spectral_kernel, dims), out_shape=(jax.S...  27.3 us
    unnamed x18, local copies, waits for them, and re-layouts  8.82 us
    pallas_call x1, Pallas kernels, fast_shards(): pl.pallas_call(functools.partial(field_kernel, 1.0 / math.sqrt(order_coun...  5.38 us

profile of v1, /device:TPU:0, one launch (start us, length us, event | category | flops | bytes accessed | tf_op | source)
XLA Modules:
  0.0 41.6 jit_solution(7168960939604505324)
XLA Ops:
  0.0 0.0 copy-start
  0.0 2.3 %copy-done = bf16[12,128,1440]{1,2,0:T(8,128)(2,1)S(1)} copy-done((bf16[12,128,1440]{1,2,0:T(8,128)(2,1)S(1)}, bf16[12,128,1440]{1,2,0:T(8,128)(2,1)}, u32[]{:S(2)}) %copy-start) | copy-done | bytes 4423704
  2.3 0.0 copy-start.1
  2.3 1.1 %copy-done.1 = bf16[2,720,192]{1,2,0:T(8,128)(2,1)S(1)} copy-done((bf16[2,720,192]{1,2,0:T(8,128)(2,1)S(1)}, bf16[2,720,192]{1,2,0:T(8,128)(2,1)}, u32[]{:S(2)}) %copy-start.1) | copy-done | bytes 552984
  3.3 0.0 copy-start.2
  3.3 1.0 %copy-done.2 = bf16[720,256]{1,0:T(8,128)(2,1)S(1)} copy-done((bf16[720,256]{1,0:T(8,128)(2,1)S(1)}, bf16[720,256]{1,0:T(8,128)(2,1)}, u32[]{:S(2)}) %copy-start.2) | copy-done | bytes 368664
  4.3 0.0 copy-start.5
  4.3 0.9 %copy-done.5 = bf16[256,256]{1,0:T(8,128)(2,1)S(1)} copy-done((bf16[256,256]{1,0:T(8,128)(2,1)S(1)}, bf16[256,256]{1,0:T(8,128)(2,1)}, u32[]{:S(2)}) %copy-start.5) | copy-done | bytes 131096
  5.2 0.0 copy-start.6
  5.2 0.9 %copy-done.6 = bf16[256,256]{1,0:T(8,128)(2,1)S(1)} copy-done((bf16[256,256]{1,0:T(8,128)(2,1)S(1)}, bf16[256,256]{1,0:T(8,128)(2,1)}, u32[]{:S(2)}) %copy-start.6) | copy-done | bytes 131096
  6.1 0.0 copy-start.7
  6.1 0.7 %copy-done.7 = s32[32]{0:T(128)S(1)} copy-done((s32[32]{0:T(128)S(1)}, s32[32]{0:T(128)}, u32[]{:S(2)}) %copy-start.7) | copy-done | bytes 152
  6.8 0.0 copy-start.8
  6.8 0.7 %copy-done.8 = f32[12]{0:T(128)S(1)} copy-done((f32[12]{0:T(128)S(1)}, f32[12]{0:T(128)}, u32[]{:S(2)}) %copy-start.8) | copy-done | bytes 72
  7.4 27.3 %spectral.1 = (bf16[12,64,128]{2,1,0:T(8,128)(2,1)S(1)}, bf16[1440,64]{1,0:T(8,128)(2,1)S(1)}) custom-call(s32[32]{0:T(128)S(1)} %copy-done.7, f32[12]{0:T(128)S(1)} %copy-done.8, bf16[12,1440,128]{2,1,0:T(8,128)(2,1)S(1)} %bitcast.3, bf16[2,192,720]{2,1,0:T(8,128)(2,1)S(1)} %bitcast.4, bf16[256,256]{1,0:T(8,128)(2,1)S(1)} %copy-done.5, ...), custom_call_target="tpu_custom_call" | custom-call | tf_op jit(solution)/shard_map/spectral/pallas_call | solution.py:367
  34.8 0.0 copy-start.3
  34.8 0.7 %copy-done.3 = bf16[1440,64]{1,0:T(8,128)(2,1)} copy-done((bf16[1440,64]{1,0:T(8,128)(2,1)}, bf16[1440,64]{1,0:T(8,128)(2,1)S(1)}, u32[]{:S(2)}) %copy-start.3) | copy-done | bytes 184344
  35.5 0.0 copy-start.4
  35.5 0.7 %copy-done.4 = bf16[12,64,128]{2,1,0:T(8,128)(2,1)} copy-done((bf16[12,64,128]{2,1,0:T(8,128)(2,1)}, bf16[12,64,128]{2,1,0:T(8,128)(2,1)S(1)}, u32[]{:S(2)}) %copy-start.4) | copy-done | bytes 196632
  36.2 5.4 %field.1 = bf16[12,1440,128]{2,1,0:T(8,128)(2,1)} custom-call(bf16[1440,64]{1,0:T(8,128)(2,1)} %copy-done.3, bf16[12,64,128]{2,1,0:T(8,128)(2,1)} %copy-done.4), custom_call_target="tpu_custom_call" | custom-call | tf_op jit(solution)/shard_map/field/pallas_call | solution.py:411
Async XLA Ops:
  0.0 2.3 %copy-start = (bf16[12,128,1440]{1,2,0:T(8,128)(2,1)S(1)}, bf16[12,128,1440]{1,2,0:T(8,128)(2,1)}, u32[]{:S(2)}) copy-start(bf16[12,128,1440]{1,2,0:T(8,128)(2,1)} %param.7) | copy-start | bytes 13271044
  2.3 1.1 %copy-start.1 = (bf16[2,720,192]{1,2,0:T(8,128)(2,1)S(1)}, bf16[2,720,192]{1,2,0:T(8,128)(2,1)}, u32[]{:S(2)}) copy-start(bf16[2,720,192]{1,2,0:T(8,128)(2,1)} %param.10) | copy-start | bytes 1658884
  3.3 1.0 %copy-start.2 = (bf16[720,256]{1,0:T(8,128)(2,1)S(1)}, bf16[720,256]{1,0:T(8,128)(2,1)}, u32[]{:S(2)}) copy-start(bf16[720,256]{1,0:T(8,128)(2,1)} %gain_hbm.1) | copy-start | bytes 1105924
  4.3 0.9 %copy-start.5 = (bf16[256,256]{1,0:T(8,128)(2,1)S(1)}, bf16[256,256]{1,0:T(8,128)(2,1)}, u32[]{:S(2)}) copy-start(bf16[256,256]{1,0:T(8,128)(2,1)} %mixr_hbm.1) | copy-start | bytes 393220
  5.2 0.9 %copy-start.6 = (bf16[256,256]{1,0:T(8,128)(2,1)S(1)}, bf16[256,256]{1,0:T(8,128)(2,1)}, u32[]{:S(2)}) copy-start(bf16[256,256]{1,0:T(8,128)(2,1)} %mixi_hbm.1) | copy-start | bytes 393220
  6.1 0.7 %copy-start.7 = (s32[32]{0:T(128)S(1)}, s32[32]{0:T(128)}, u32[]{:S(2)}) copy-start(s32[32]{0:T(128)} %orders_ref.1) | copy-start | bytes 388
  6.8 0.7 %copy-start.8 = (f32[12]{0:T(128)S(1)}, f32[12]{0:T(128)}, u32[]{:S(2)}) copy-start(f32[12]{0:T(128)} %quad_ref.1) | copy-start | bytes 148
  34.8 0.7 %copy-start.3 = (bf16[1440,64]{1,0:T(8,128)(2,1)}, bf16[1440,64]{1,0:T(8,128)(2,1)S(1)}, u32[]{:S(2)}) copy-start(bf16[1440,64]{1,0:T(8,128)(2,1)S(1)} %get-tuple-element.7.tabt_ref) | copy-start | bytes 552964
  35.5 0.7 %copy-start.4 = (bf16[12,64,128]{2,1,0:T(8,128)(2,1)}, bf16[12,64,128]{2,1,0:T(8,128)(2,1)S(1)}, u32[]{:S(2)}) copy-start(bf16[12,64,128]{2,1,0:T(8,128)(2,1)S(1)} %get-tuple-element.8.syn_ref) | copy-start | bytes 589828

commit v2 on v1

--- a/solution.py
+++ b/solution.py
@@ -93,10 +93,10 @@
 
 
 def spectral_kernel(
-    dims, orders_ref, quad_ref, grid_hbm, leg_hbm, mixr_hbm, mixi_hbm, gain_hbm,
+    dims, orders_hbm, quad_hbm, grid_hbm, leg_hbm, mixr_hbm, mixi_hbm, gain_hbm,
     out_ref, tabt_ref,
     grid_v, leg_v, mixr_v, mixi_v, gain_v, tab, spread_a, spread_b, send1, recv1, lt, lf,
-    weight, mixed, send2, recv2, flat2,
+    weight, mixed, send2, recv2, flat2, orders_ref, quad_ref,
     grid_sem, in_sem, local_sem, s_send, s_recv, f_send, f_recv, b_send, b_recv,
 ):
     n_wide, lat_dev, lon_count, chan, m_dev, deg_count = dims
@@ -110,6 +110,11 @@
     x = lax.axis_index("narrow")
     partner = 1 - x
 
+    scalar_copies = []
+    for i, (src, dst) in enumerate(((orders_hbm, orders_ref), (quad_hbm, quad_ref))):
+        copy = pltpu.make_async_copy(src, dst, in_sem.at[4 + i])
+        copy.start()
+        scalar_copies.append(copy)
     grid_copies = []
     for p in range(pairs):
         copy = pltpu.make_async_copy(
@@ -132,6 +137,8 @@
         )
     pl.semaphore_signal(barrier, inc=1, device_id=(me, partner), device_id_type=MESH)
 
+    for copy in scalar_copies:
+        copy.wait()
     row = lax.broadcasted_iota(jnp.int32, (rows, LANES), 0)
     lane = lax.broadcasted_iota(jnp.int32, (rows, LANES), 1)
     block_rows = 2 * n_wide
@@ -342,7 +349,8 @@
 
 
 def field_kernel(scale, chan, tabt_ref, syn_ref, out_ref):
-    rhs = jnp.concatenate([syn_ref[0], syn_ref[1]], axis=1)
+    p = pl.program_id(0)
+    rhs = jnp.concatenate([syn_ref[2 * p], syn_ref[2 * p + 1]], axis=1)
     res = jnp.dot(tabt_ref[...], rhs, preferred_element_type=jnp.float32) * scale
     res = res.astype(jnp.bfloat16)
     out_ref[0] = res[:, :chan]
@@ -359,8 +367,7 @@
     half = n_wide * SUB
     bf16, f32 = jnp.bfloat16, jnp.float32
     vmem = pl.BlockSpec(memory_space=pltpu.VMEM)
-    smem = pl.BlockSpec(memory_space=pltpu.SMEM)
-    hbm = pl.BlockSpec(memory_space=pl.ANY)
+    hbm = pl.BlockSpec(memory_space=pltpu.HBM)
     dims = (n_wide, lat_dev, lon_count, chan, m_dev, deg_count)
     chan_all = mix_real.shape[0]
     dma = pltpu.SemaphoreType.DMA
@@ -370,7 +377,7 @@
             jax.ShapeDtypeStruct((lat_dev, rows, chan), bf16),
             jax.ShapeDtypeStruct((lon_count, rows), bf16),
         ),
-        in_specs=[smem, smem, hbm, hbm, hbm, hbm, hbm],
+        in_specs=[hbm] * 7,
         out_specs=(vmem, vmem),
         scratch_shapes=[
             pltpu.VMEM((lat_dev, lon_count, chan), bf16),
@@ -390,8 +397,10 @@
             pltpu.VMEM((n_wide, parts, SUB, 2 * chan), bf16),
             pltpu.VMEM((n_wide, parts, SUB, 2 * chan), bf16),
             pltpu.VMEM((2, n_wide * parts * SUB, chan), f32),
+            pltpu.SMEM((order_count,), jnp.int32),
+            pltpu.SMEM((lat_dev,), f32),
             dma((lat_dev // 2,)),
-            dma((4,)),
+            dma((6,)),
             dma((3,)),
             dma((2, n_wide)),
             dma((2, n_wide)),
@@ -404,19 +413,17 @@
             collective_id=0, has_side_effects=True, vmem_limit_bytes=40 * 2**20
         ),
         name="spectral",
-    )(
+    )(*(pltpu.with_memory_space_constraint(v, pltpu.HBM) for v in (
         orders, quad_weights, jnp.transpose(grid, (0, 2, 1)), jnp.transpose(legendre, (0, 2, 1)),
         mix_real, mix_imag, filter_gain,
-    )
+    )))
     field = pl.pallas_call(
         functools.partial(field_kernel, 1.0 / math.sqrt(order_count), chan),
         grid=(lat_dev // 2,),
         out_shape=jax.ShapeDtypeStruct((lat_dev, lon_count, chan), bf16),
-        in_specs=[
-            pl.BlockSpec((lon_count, rows), lambda p: (0, 0)),
-            pl.BlockSpec((2, rows, chan), lambda p: (p, 0, 0)),
-        ],
+        in_specs=[vmem, vmem],
         out_specs=pl.BlockSpec((2, lon_count, chan), lambda p: (p, 0, 0)),
+        compiler_params=pltpu.CompilerParams(vmem_limit_bytes=16 * 2**20),
         name="field",
     )(table, synthesis)
     return jnp.transpose(field, (0, 2, 1))

time: 42.1 us -> 28.4 us (0.67); the launches traced: 41.6 us -> 28.3 us
  local copies, waits for them, and re-layouts: 8.82 us -> 0 us
  Pallas kernels: 32.7 us -> 28.3 us
    unnamed x18 -> x0, local copies, waits for them, and re-layouts: 8.82 us -> none
    pallas_call x1, Pallas kernels: 27.3 us -> 24.3 us  [fast_shards(): pl.pallas_call(functools.partial(spectral_kernel, dims), out_shape=(jax.S...]
    pallas_call x1, Pallas kernels: 5.38 us -> 3.95 us  [fast_shards(): pl.pallas_call(functools.partial(field_kernel, 1.0 / math.sqrt(order_coun...]
where the time goes in v2:
time: 28.4 us; the launch traced here: 28.3 us
  Pallas kernels  28.3 us (100%)
    pallas_call x1, Pallas kernels, fast_shards(): pl.pallas_call(functools.partial(spectral_kernel, dims), out_shape=(jax.S...  24.3 us
    pallas_call x1, Pallas kernels, fast_shards(): pl.pallas_call(functools.partial(field_kernel, 1.0 / math.sqrt(order_coun...  3.95 us

profile of v2, /device:TPU:0, one launch (start us, length us, event | category | flops | bytes accessed | tf_op | source)
XLA Modules:
  0.0 28.3 jit_solution(7478753791227057142)
XLA Ops:
  0.0 24.3 %spectral.1 = (bf16[12,64,128]{2,1,0:T(8,128)(2,1)S(1)}, bf16[1440,64]{1,0:T(8,128)(2,1)S(1)}) custom-call(s32[32]{0:T(128)} %orders_hbm.1, f32[12]{0:T(128)} %quad_hbm.1, bf16[12,1440,128]{2,1,0:T(8,128)(2,1)} %bitcast.3, bf16[2,192,720]{2,1,0:T(8,128)(2,1)} %bitcast.4, bf16[256,256]{1,0:T(8,128)(2,1)} %mixr_hbm.1, bf16[256,256]{1,0:T(8,128)(2,1)} %mixi_hbm.1, ...), custom_call_target="tpu_custom_call" | custom-call | tf_op jit(solution)/shard_map/spectral/pallas_call | solution.py:374
  24.3 3.9 %field.1 = bf16[12,1440,128]{2,1,0:T(8,128)(2,1)} custom-call(bf16[1440,64]{1,0:T(8,128)(2,1)S(1)} %get-tuple-element.7.tabt_ref, bf16[12,64,128]{2,1,0:T(8,128)(2,1)S(1)} %get-tuple-element.8.syn_ref), custom_call_target="tpu_custom_call" | custom-call | tf_op jit(solution)/shard_map/field/pallas_call | solution.py:420

commit v3 on v2

--- a/solution.py
+++ b/solution.py
@@ -96,7 +96,7 @@
     dims, orders_hbm, quad_hbm, grid_hbm, leg_hbm, mixr_hbm, mixi_hbm, gain_hbm,
     out_ref, tabt_ref,
     grid_v, leg_v, mixr_v, mixi_v, gain_v, tab, spread_a, spread_b, send1, recv1, lt, lf,
-    weight, mixed, send2, recv2, flat2, orders_ref, quad_ref,
+    weight, coeffs, mixed, send2, recv2, flat2, orders_ref, quad_ref,
     grid_sem, in_sem, local_sem, s_send, s_recv, f_send, f_recv, b_send, b_recv,
 ):
     n_wide, lat_dev, lon_count, chan, m_dev, deg_count = dims
@@ -122,6 +122,23 @@
         )
         copy.start()
         grid_copies.append(copy)
+    half_w = n_wide // 2
+    base = (me // half_w) * half_w
+    spot = me % half_w
+
+    def near(i):
+        return base + (spot + i) % half_w
+
+    def far(i):
+        return half_w - base + (spot + i) % half_w
+
+    barrier = pltpu.get_barrier_semaphore()
+    targets = [(far(i), x) for i in range(half_w)]
+    targets += [(near(i), partner) for i in range(half_w)]
+    targets += [(near(i), x) for i in range(1, half_w)]
+    for target in targets:
+        pl.semaphore_signal(barrier, inc=1, device_id=target, device_id_type=MESH)
+
     in_copies = []
     for i, (src, dst) in enumerate(
         ((leg_hbm, leg_v), (mixr_hbm, mixr_v), (mixi_hbm, mixi_v), (gain_hbm, gain_v))
@@ -129,13 +146,6 @@
         copy = pltpu.make_async_copy(src, dst, in_sem.at[i])
         copy.start()
         in_copies.append(copy)
-
-    barrier = pltpu.get_barrier_semaphore()
-    for d in range(1, n_wide):
-        pl.semaphore_signal(
-            barrier, inc=1, device_id=((me + d) % n_wide, x), device_id_type=MESH
-        )
-    pl.semaphore_signal(barrier, inc=1, device_id=(me, partner), device_id_type=MESH)
 
     for copy in scalar_copies:
         copy.wait()
@@ -175,44 +185,68 @@
                     at = (j * rest + a - SUB) * block_rows
                     spread_b[at:at + block_rows, :] = part[j * block_rows:(j + 1) * block_rows]
 
-    def wide_copy(part, d):
-        to = (me + d) % n_wide
-        where = pl.ds(0, m_dev) if part == 0 else pl.ds(m_dev, 1)
-        return pltpu.make_async_remote_copy(
-            src_ref=send1.at[to, where],
-            dst_ref=recv1.at[0, me, where],
-            send_sem=s_send.at[part, d],
+    def span(part):
+        return pl.ds(0, m_dev) if part == 0 else pl.ds(m_dev, 1)
+
+    def wide_copy(part, to, sem):
+        return pltpu.make_async_remote_copy(
+            src_ref=send1.at[to, span(part)],
+            dst_ref=recv1.at[0, me, span(part)],
+            send_sem=s_send.at[part, sem],
             recv_sem=s_recv.at[part, me],
             device_id=(to, x),
             device_id_type=MESH,
         )
 
+    def cross_copy(part, i):
+        return pltpu.make_async_remote_copy(
+            src_ref=send1.at[near(i), span(part)],
+            dst_ref=recv1.at[1, me, span(part)],
+            send_sem=f_send.at[part, i],
+            recv_sem=f_recv.at[part, me],
+            device_id=(near(i), partner),
+            device_id_type=MESH,
+        )
+
     def wide_arrival(part, src):
-        where = pl.ds(0, m_dev) if part == 0 else pl.ds(m_dev, 1)
-        return pltpu.make_async_remote_copy(
-            src_ref=send1.at[src, where],
-            dst_ref=recv1.at[0, src, where],
+        return pltpu.make_async_remote_copy(
+            src_ref=send1.at[src, span(part)],
+            dst_ref=recv1.at[0, src, span(part)],
             send_sem=s_send.at[part, 0],
             recv_sem=s_recv.at[part, src],
             device_id=(src, x),
             device_id_type=MESH,
         )
 
-    def forward_copy(part, src):
-        where = pl.ds(0, m_dev) if part == 0 else pl.ds(m_dev, 1)
-        return pltpu.make_async_remote_copy(
-            src_ref=recv1.at[0, src, where],
-            dst_ref=recv1.at[1, src, where],
-            send_sem=f_send.at[part, src],
+    def forward_copy(part, i):
+        return pltpu.make_async_remote_copy(
+            src_ref=recv1.at[0, far(i), span(part)],
+            dst_ref=recv1.at[1, far(i), span(part)],
+            send_sem=f_send.at[part, half_w + i],
+            recv_sem=f_recv.at[part, far(i)],
+            device_id=(me, partner),
+            device_id_type=MESH,
+        )
+
+    def partner_arrival(part, src):
+        return pltpu.make_async_remote_copy(
+            src_ref=recv1.at[0, src, span(part)],
+            dst_ref=recv1.at[1, src, span(part)],
+            send_sem=f_send.at[part, 0],
             recv_sem=f_recv.at[part, src],
             device_id=(me, partner),
             device_id_type=MESH,
         )
 
+    def out_copies(part):
+        copies = [wide_copy(part, far(i), i) for i in range(half_w)]
+        copies += [cross_copy(part, i) for i in range(half_w)]
+        copies += [wide_copy(part, near(i), half_w + i) for i in range(1, half_w)]
+        return copies
+
     def own_copy(part):
-        where = pl.ds(0, m_dev) if part == 0 else pl.ds(m_dev, 1)
         return pltpu.make_async_copy(
-            send1.at[me, where], recv1.at[0, me, where], local_sem.at[part]
+            send1.at[me, span(part)], recv1.at[0, me, span(part)], local_sem.at[part]
         )
 
     for p in range(SUB // 2):
@@ -224,9 +258,9 @@
                 send1[w, j, :, ri * chan:(ri + 1) * chan] = spread_a[
                     pl.ds(at, SUB, stride=rows), :
                 ].astype(jnp.bfloat16)
-    pl.semaphore_wait(barrier, n_wide)
-    for d in range(1, n_wide):
-        wide_copy(0, d).start()
+    pl.semaphore_wait(barrier, len(targets))
+    for copy in out_copies(0):
+        copy.start()
     own_copy(0).start()
 
     for p in range(SUB // 2, pairs):
@@ -236,12 +270,9 @@
             send1[w, m_dev, :, ri * chan:(ri + 1) * chan] = spread_b[
                 pl.ds(ri * n_wide + w, SUB, stride=block_rows), :
             ].astype(jnp.bfloat16)
-    for d in range(1, n_wide):
-        wide_copy(1, d).start()
+    for copy in out_copies(1):
+        copy.start()
     own_copy(1).start()
-    for part in range(2):
-        own_copy(part).wait()
-        forward_copy(part, me).start()
 
     for copy in in_copies:
         copy.wait()
@@ -273,85 +304,113 @@
         weight[top + chan:top + 2 * chan, chan:] = re
 
     for part in range(2):
-        for d in range(1, n_wide):
-            src = (me + n_wide - d) % n_wide
-            wide_arrival(part, src).wait_recv()
-            forward_copy(part, src).start()
+        for i in range(half_w):
+            wide_arrival(part, far(i)).wait_recv()
+            forward_copy(part, i).start()
     for part in range(2):
-        for d in range(n_wide):
-            forward_copy(part, (me + n_wide - d) % n_wide).wait_recv()
+        own_copy(part).wait()
+        for i in range(1, half_w):
+            wide_arrival(part, near(i)).wait_recv()
+
+    def transform_lat(side, j):
+        head = recv1[side, :, j].reshape(half, 2 * chan)
+        tail = recv1[side, :, m_dev].reshape(half, 2 * chan)
+        spec = jnp.concatenate([head, tail], axis=0)
+        res = jnp.dot(lf[j], spec, preferred_element_type=jnp.float32)
+        coeffs[j, :, 2 * side * chan:2 * (side + 1) * chan] = res.astype(jnp.bfloat16)
+
+    for j in range(m_dev):
+        transform_lat(0, j)
+    for part in range(2):
+        for i in range(half_w):
+            partner_arrival(part, near(i)).wait_recv()
+        for i in range(half_w):
+            partner_arrival(part, far(i)).wait_recv()
 
     gain = gain_v[:, own_cols].astype(jnp.float32)
     gain = jnp.concatenate([gain, gain], axis=1)
+
+    def back_copy(part, to, sem):
+        where = pl.ds(0, 1) if part == 0 else pl.ds(1, parts - 1)
+        return pltpu.make_async_remote_copy(
+            src_ref=send2.at[to, where],
+            dst_ref=recv2.at[me, where],
+            send_sem=b_send.at[part, sem],
+            recv_sem=b_recv.at[part, me],
+            device_id=(to, x),
+            device_id_type=MESH,
+        )
+
+    def back_arrival(part, src):
+        where = pl.ds(0, 1) if part == 0 else pl.ds(1, parts - 1)
+        return pltpu.make_async_remote_copy(
+            src_ref=send2.at[src, where],
+            dst_ref=recv2.at[src, where],
+            send_sem=b_send.at[part, 0],
+            recv_sem=b_recv.at[part, src],
+            device_id=(src, x),
+            device_id_type=MESH,
+        )
+
+    def back_copies(part):
+        copies = [back_copy(part, far(i), i) for i in range(half_w)]
+        return copies + [back_copy(part, near(i), half_w + i) for i in range(1, half_w)]
+
     tails = []
     for j in range(m_dev):
-        sides = []
-        for side in range(2):
-            head = recv1[side, :, j].reshape(half, 2 * chan)
-            tail = recv1[side, :, m_dev].reshape(half, 2 * chan)
-            sides.append(jnp.concatenate([head, tail], axis=0))
-        spec = jnp.concatenate(sides, axis=1)
-        coeffs = jnp.dot(lf[j], spec, preferred_element_type=jnp.float32).astype(jnp.bfloat16)
-        product = jnp.dot(coeffs, weight[...], preferred_element_type=jnp.float32)
+        transform_lat(1, j)
+        product = jnp.dot(coeffs[j], weight[...], preferred_element_type=jnp.float32)
         mixed[j] = (product * gain).astype(jnp.bfloat16)
         syn = jnp.dot(lt[j], mixed[j], preferred_element_type=jnp.float32)
         send2[:, j] = syn[:half].astype(jnp.bfloat16).reshape(n_wide, SUB, 2 * chan)
         tails.append(syn[half:])
+        if j == 0:
+            for copy in back_copies(0):
+                copy.start()
     total = functools.reduce(lambda a, b: a + b, tails)
     send2[:, m_dev] = total.astype(jnp.bfloat16).reshape(n_wide, SUB, 2 * chan)
-
-    def back_copy(to, d):
-        return pltpu.make_async_remote_copy(
-            src_ref=send2.at[to],
-            dst_ref=recv2.at[me],
-            send_sem=b_send.at[d],
-            recv_sem=b_recv.at[me],
-            device_id=(to, x),
-            device_id_type=MESH,
-        )
-
-    def back_arrival(src):
-        return pltpu.make_async_remote_copy(
-            src_ref=send2.at[src],
-            dst_ref=recv2.at[src],
-            send_sem=b_send.at[0],
-            recv_sem=b_recv.at[src],
-            device_id=(src, x),
-            device_id_type=MESH,
-        )
-
-    for d in range(1, n_wide):
-        back_copy((me + d) % n_wide, d).start()
-    own_back = pltpu.make_async_copy(send2.at[me], recv2.at[me], local_sem.at[2])
-    own_back.start()
+    for copy in back_copies(1):
+        copy.start()
+
+    stride = parts * SUB
+
+    def widen(src, ref):
+        at = pl.ds(pl.multiple_of(src * stride, SUB), stride)
+        block = ref[src]
+        for ri in range(2):
+            flat2[ri, at, :] = block[:, :, ri * chan:(ri + 1) * chan].astype(
+                jnp.float32
+            ).reshape(stride, chan)
+
+    widen(me, send2)
     for part in range(2):
-        for d in range(1, n_wide):
-            wide_copy(part, d).wait_send()
-        for d in range(n_wide):
-            forward_copy(part, (me + n_wide - d) % n_wide).wait_send()
-    own_back.wait()
-    for d in range(1, n_wide):
-        back_arrival((me + n_wide - d) % n_wide).wait_recv()
-    for ri in range(2):
-        flat2[ri] = recv2[:, :, :, ri * chan:(ri + 1) * chan].astype(jnp.float32).reshape(
-            n_wide * parts * SUB, chan
-        )
+        for copy in out_copies(part):
+            copy.wait_send()
+        for i in range(half_w):
+            forward_copy(part, i).wait_send()
+    for src in [near(i) for i in range(1, half_w)] + [far(i) for i in range(half_w)]:
+        for part in range(2):
+            back_arrival(part, src).wait_recv()
+        widen(src, recv2)
     for a in range(lat_dev):
         for j in range(m_dev):
             for ri in range(2):
                 at = j * SUB + a if a < SUB else m_dev * SUB + j * rest + a - SUB
                 top = j * block_rows + ri * n_wide
                 out_ref[a, top:top + n_wide, :] = flat2[
-                    ri, pl.ds(at, n_wide, stride=parts * SUB), :
+                    ri, pl.ds(at, n_wide, stride=stride), :
                 ].astype(jnp.bfloat16)
-    for d in range(1, n_wide):
-        back_copy((me + d) % n_wide, d).wait_send()
+    for part in range(2):
+        for copy in back_copies(part):
+            copy.wait_send()
 
 
 def field_kernel(scale, chan, tabt_ref, syn_ref, out_ref):
     p = pl.program_id(0)
+    count = out_ref.shape[1]
+    lons = pl.ds(pl.multiple_of(pl.program_id(1) * count, 16), count)
     rhs = jnp.concatenate([syn_ref[2 * p], syn_ref[2 * p + 1]], axis=1)
-    res = jnp.dot(tabt_ref[...], rhs, preferred_element_type=jnp.float32) * scale
+    res = jnp.dot(tabt_ref[lons, :], rhs, preferred_element_type=jnp.float32) * scale
     res = res.astype(jnp.bfloat16)
     out_ref[0] = res[:, :chan]
     out_ref[1] = res[:, chan:]
@@ -393,6 +452,7 @@
             pltpu.VMEM((m_dev, 2 * half, deg_count), bf16),
             pltpu.VMEM((m_dev, deg_count, 2 * half), bf16),
             pltpu.VMEM((4 * chan, 2 * chan), bf16),
+            pltpu.VMEM((m_dev, deg_count, 4 * chan), bf16),
             pltpu.VMEM((m_dev, deg_count, 2 * chan), bf16),
             pltpu.VMEM((n_wide, parts, SUB, 2 * chan), bf16),
             pltpu.VMEM((n_wide, parts, SUB, 2 * chan), bf16),
@@ -401,13 +461,13 @@
             pltpu.SMEM((lat_dev,), f32),
             dma((lat_dev // 2,)),
             dma((6,)),
-            dma((3,)),
+            dma((2,)),
             dma((2, n_wide)),
             dma((2, n_wide)),
             dma((2, n_wide)),
             dma((2, n_wide)),
-            dma((n_wide,)),
-            dma((n_wide,)),
+            dma((2, n_wide)),
+            dma((2, n_wide)),
         ],
         compiler_params=pltpu.CompilerParams(
             collective_id=0, has_side_effects=True, vmem_limit_bytes=40 * 2**20
@@ -419,10 +479,10 @@
     )))
     field = pl.pallas_call(
         functools.partial(field_kernel, 1.0 / math.sqrt(order_count), chan),
-        grid=(lat_dev // 2,),
+        grid=(lat_dev // 2, 2),
         out_shape=jax.ShapeDtypeStruct((lat_dev, lon_count, chan), bf16),
         in_specs=[vmem, vmem],
-        out_specs=pl.BlockSpec((2, lon_count, chan), lambda p: (p, 0, 0)),
+        out_specs=pl.BlockSpec((2, lon_count // 2, chan), lambda p, h: (p, h, 0)),
         compiler_params=pltpu.CompilerParams(vmem_limit_bytes=16 * 2**20),
         name="field",
     )(table, synthesis)
@@ -437,7 +497,7 @@
     fits = (
         lax.axis_size("narrow") == 2
         and chan == LANES
-        and lon_count % 4 == 0
+        and lon_count % 32 == 0
         and rest > 0
         and rest * m_dev == SUB
         and lat_dev % 2 == 0

time: 28.4 us -> 31.7 us (1.12)
  Pallas kernels: 28.3 us -> 31.6 us
    pallas_call x1, Pallas kernels: 3.95 us -> 6.12 us  [fast_shards(): pl.pallas_call(functools.partial(field_kernel, 1.0 / math.sqrt(order_coun...]
    pallas_call x1, Pallas kernels: 24.3 us -> 25.5 us  [fast_shards(): pl.pallas_call(functools.partial(spectral_kernel, dims), out_shape=(jax.S...]
where the time goes in v3:
time: 31.7 us; the launch traced here: 31.6 us
  Pallas kernels  31.6 us (100%)
    pallas_call x1, Pallas kernels, fast_shards(): pl.pallas_call(functools.partial(spectral_kernel, dims), out_shape=(jax.S...  25.5 us
    pallas_call x1, Pallas kernels, fast_shards(): pl.pallas_call(functools.partial(field_kernel, 1.0 / math.sqrt(order_coun...  6.12 us

profile of v3, /device:TPU:0, one launch (start us, length us, event | category | flops | bytes accessed | tf_op | source)
XLA Modules:
  0.0 31.6 jit_solution(2893307895530184343)
XLA Ops:
  0.0 25.5 %spectral.1 = (bf16[12,64,128]{2,1,0:T(8,128)(2,1)S(1)}, bf16[1440,64]{1,0:T(8,128)(2,1)S(1)}) custom-call(s32[32]{0:T(128)} %orders_hbm.1, f32[12]{0:T(128)} %quad_hbm.1, bf16[12,1440,128]{2,1,0:T(8,128)(2,1)} %bitcast.3, bf16[2,192,720]{2,1,0:T(8,128)(2,1)} %bitcast.4, bf16[256,256]{1,0:T(8,128)(2,1)} %mixr_hbm.1, bf16[256,256]{1,0:T(8,128)(2,1)} %mixi_hbm.1, ...), custom_call_target="tpu_custom_call" | custom-call | tf_op jit(solution)/shard_map/spectral/pallas_call | solution.py:433
  25.5 6.1 %field.1 = bf16[12,1440,128]{2,1,0:T(8,128)(2,1)} custom-call(bf16[1440,64]{1,0:T(8,128)(2,1)S(1)} %get-tuple-element.7.tabt_ref, bf16[12,64,128]{2,1,0:T(8,128)(2,1)S(1)} %get-tuple-element.8.syn_ref), custom_call_target="tpu_custom_call" | custom-call | tf_op jit(solution)/shard_map/field/pallas_call | solution.py:480

commit v4 on v2

--- a/solution.py
+++ b/solution.py
@@ -348,13 +348,21 @@
         back_copy((me + d) % n_wide, d).wait_send()
 
 
-def field_kernel(scale, chan, tabt_ref, syn_ref, out_ref):
-    p = pl.program_id(0)
-    rhs = jnp.concatenate([syn_ref[2 * p], syn_ref[2 * p + 1]], axis=1)
-    res = jnp.dot(tabt_ref[...], rhs, preferred_element_type=jnp.float32) * scale
-    res = res.astype(jnp.bfloat16)
-    out_ref[0] = res[:, :chan]
-    out_ref[1] = res[:, chan:]
+def field_kernel(scale, tabt_ref, syn_ref, out_hbm, held, sem):
+    lat_dev, _, chan = held.shape
+    copies = []
+    for p in range(lat_dev // 2):
+        rhs = jnp.concatenate([syn_ref[2 * p], syn_ref[2 * p + 1]], axis=1)
+        res = jnp.dot(tabt_ref[...], rhs, preferred_element_type=jnp.float32) * scale
+        res = res.astype(jnp.bfloat16)
+        held[2 * p] = res[:, :chan]
+        held[2 * p + 1] = res[:, chan:]
+        both = pl.ds(2 * p, 2)
+        copy = pltpu.make_async_copy(held.at[both], out_hbm.at[both], sem.at[p])
+        copy.start()
+        copies.append(copy)
+    for copy in copies:
+        copy.wait()
 
 
 def fast_shards(grid, quad_weights, orders, legendre, mix_real, mix_imag, filter_gain):
@@ -418,12 +426,12 @@
         mix_real, mix_imag, filter_gain,
     )))
     field = pl.pallas_call(
-        functools.partial(field_kernel, 1.0 / math.sqrt(order_count), chan),
-        grid=(lat_dev // 2,),
+        functools.partial(field_kernel, 1.0 / math.sqrt(order_count)),
         out_shape=jax.ShapeDtypeStruct((lat_dev, lon_count, chan), bf16),
         in_specs=[vmem, vmem],
-        out_specs=pl.BlockSpec((2, lon_count, chan), lambda p: (p, 0, 0)),
-        compiler_params=pltpu.CompilerParams(vmem_limit_bytes=16 * 2**20),
+        out_specs=pl.BlockSpec(memory_space=pl.ANY),
+        scratch_shapes=[pltpu.VMEM((lat_dev, lon_count, chan), bf16), dma((lat_dev // 2,))],
+        compiler_params=pltpu.CompilerParams(vmem_limit_bytes=24 * 2**20),
         name="field",
     )(table, synthesis)
     return jnp.transpose(field, (0, 2, 1))

time: 28.4 us -> 27.1 us (0.954)
  Pallas kernels: 28.3 us -> 27 us
    pallas_call x1, Pallas kernels: 3.95 us -> 2.65 us  [fast_shards(): pl.pallas_call(functools.partial(field_kernel, 1.0 / math.sqrt(order_coun...]
where the time goes in v4:
time: 27.1 us; the launch traced here: 27 us
  Pallas kernels  27 us (100%)
    pallas_call x1, Pallas kernels, fast_shards(): pl.pallas_call(functools.partial(spectral_kernel, dims), out_shape=(jax.S...  24.3 us
    pallas_call x1, Pallas kernels, fast_shards(): pl.pallas_call(functools.partial(field_kernel, 1.0 / math.sqrt(order_coun...  2.65 us

profile of v4, /device:TPU:0, one launch (start us, length us, event | category | flops | bytes accessed | tf_op | source)
XLA Modules:
  0.0 27.0 jit_solution(8236156268042806514)
XLA Ops:
  0.0 24.3 %spectral.1 = (bf16[12,64,128]{2,1,0:T(8,128)(2,1)S(1)}, bf16[1440,64]{1,0:T(8,128)(2,1)S(1)}) custom-call(s32[32]{0:T(128)} %orders_hbm.1, f32[12]{0:T(128)} %quad_hbm.1, bf16[12,1440,128]{2,1,0:T(8,128)(2,1)} %bitcast.3, bf16[2,192,720]{2,1,0:T(8,128)(2,1)} %bitcast.4, bf16[256,256]{1,0:T(8,128)(2,1)} %mixr_hbm.1, bf16[256,256]{1,0:T(8,128)(2,1)} %mixi_hbm.1, ...), custom_call_target="tpu_custom_call" | custom-call | tf_op jit(solution)/shard_map/spectral/pallas_call | solution.py:382
  24.3 2.6 %field.1 = bf16[12,1440,128]{2,1,0:T(8,128)(2,1)} custom-call(bf16[1440,64]{1,0:T(8,128)(2,1)S(1)} %get-tuple-element.7.tabt_ref, bf16[12,64,128]{2,1,0:T(8,128)(2,1)S(1)} %get-tuple-element.8.syn_ref), custom_call_target="tpu_custom_call" | custom-call | tf_op jit(solution)/shard_map/field/pallas_call | solution.py:428
